TPU v7x, 32 devices: a whole 2x2x4 slice. The times are simulated.
32 devices in a mesh: region: 2 (over y), space: 8 (over z, x), day: 2 (over core).
Axes of the slice: x: 2, y: 2, z: 4, core: 2. Of those that a mesh axis runs over, the one named last changes fastest.
Arguments:
- observed: float32 [4, 64, 4096], P('day', ('region', 'space')), parts along dimension 1, may hold values from -20 to 20
- gap_mask: int32 [4, 64, 4096], P('day', ('region', 'space')), parts along dimension 1, may hold values 0 or 1
- sea_mask: int32 [64, 4096], P(('region', 'space')), parts along dimension 0, may hold values 0 or 1
- stencil: bfloat16 [9, 64, 4096], P(None, ('region', 'space')), parts along dimension 1, may hold values from 0.019897461 to 0.19921875
- precision: float32 [64, 4096], P(('region', 'space')), parts along dimension 0, may hold values from 0.5 to 4
- noise_precision: float32 [64, 4096], P(('region', 'space')), parts along dimension 0, may hold values from 0.5 to 8
- perturbation: bfloat16 [2, 4, 64, 4096], P(None, 'day', ('region', 'space')), parts along dimension 2, may hold values from -6 to 6
Outputs:
- posterior_mean: float32 [4, 64, 4096], P('day', ('region', 'space')), parts along dimension 1
- fitted: float32 [2, 64, 4096], P(None, ('region', 'space'), 'day'), parts along dimension 1
There are 2 independent parts, one for each index of `region`. A program takes and returns all parts, laid end to end along the dimension named above; each array names one. Nothing has to cross between parts.
All inputs are finite; a program needn't handle non-finite values. No bound on the sum of `gap_mask` or of `sea_mask` on one device may be relied on, other than what follows from the above.
Results may differ from a plain program's by a relative error of at most 0.0003.
Values sent between devices are 32-bit elements; how exact they have to be, the bound alone decides.
No kernel may reach another device: no remote copies, remote signals or barrier semaphores. Data moves between devices by JAX's collectives and lax.ppermute only.
A program may use at most 64 MiB of HBM per device.

v0:
```python
import jax
import jax.numpy as jnp
from jax import lax
from jax.sharding import PartitionSpec as P

ITERS = 2
OFFSETS = ((-1, -1), (-1, 0), (-1, 1), (0, -1), (0, 0), (0, 1), (1, -1), (1, 0), (1, 1))
RIDGE = 1.0


def padded(x, sides, width):
    for axis, dim in sides:
        size, length = (lax.axis_size(axis), x.shape[dim])
        up = [(i, (i + 1) % size) for i in range(size - 1)]
        down = [(j, i) for i, j in up]
        last = lax.slice_in_dim(x, length - width, length, axis=dim)
        first = lax.slice_in_dim(x, 0, width, axis=dim)
        before = lax.ppermute(last, axis, up)
        after = lax.ppermute(first, axis, down)
        x = jnp.concatenate([before, x, after], axis=dim)
    return x


def from_behind(x, axis, by):
    size = lax.axis_size(axis)
    pairs = [(i, i + by) for i in range(size) if 0 <= i + by < size]
    return lax.ppermute(x, axis, pairs)


def column_shift(values, col_step):
    if col_step == 0:
        return values
    zero_column = jnp.zeros_like(values[..., :1])
    if col_step > 0:
        return jnp.concatenate([values[..., 1:], zero_column], -1)
    return jnp.concatenate([zero_column, values[..., :-1]], -1)


def forward_rows(values, coefficients):
    height = coefficients.shape[1]
    result = jnp.zeros(values[..., 1:-1, :].shape, jnp.float32)
    for position, (row_step, col_step) in enumerate(OFFSETS):
        rows_taken = values[..., 1 + row_step : 1 + row_step + height, :]
        result = result + coefficients[position] * column_shift(rows_taken, col_step)
    return result


def transposed_rows(values, coefficients):
    height = values.shape[-2] - 2
    result = jnp.zeros(values[..., 1:-1, :].shape, jnp.float32)
    for position, (row_step, col_step) in enumerate(OFFSETS):
        product = coefficients[position] * values
        rows_taken = product[..., 1 - row_step : 1 - row_step + height, :]
        result = result + column_shift(rows_taken, -col_step)
    return result


def local_sums(first, second):
    return jnp.sum(first * second, axis=(1, 2, 3))


def expand(scalars):
    return scalars[:, None, None, None]


def fit_cells(totals):
    diag_first = totals[0] + RIDGE
    cross_term = totals[1]
    diag_second = totals[2] + RIDGE
    determinant = diag_first * diag_second - cross_term * cross_term
    persistence = (diag_second * totals[3] - cross_term * totals[4]) / determinant
    diffusion = (diag_first * totals[4] - cross_term * totals[3]) / determinant
    return jnp.stack([persistence, diffusion], 0)


def shards(observed, gap_mask, sea_mask, stencil, precision, noise_precision, perturbation):
    sea_float = sea_mask.astype(jnp.float32)
    coefficients = stencil.astype(jnp.float32)
    observed_precision = noise_precision * gap_mask.astype(jnp.float32)
    base_side = sea_float * observed_precision * observed
    spread = sea_float * jnp.sqrt(precision + observed_precision)
    right_sides = jnp.stack(
        [
            base_side,
            base_side + spread * perturbation[0].astype(jnp.float32),
            base_side + spread * perturbation[1].astype(jnp.float32),
        ],
        0,
    )
    static_rim = padded(coefficients, (("space", 1),), 1)
    day_number = lax.axis_index("day")
    day_total = lax.axis_size("day")

    def residual_norms(residual):
        return lax.psum(local_sums(residual, residual), ("space", "day"))

    solution = jnp.zeros_like(right_sides)
    residual = right_sides
    direction = right_sides
    norm_now = residual_norms(residual)
    for iteration in range(ITERS):
        masked = sea_float * direction
        padded_state = padded(masked, (("space", 2),), 1)
        apply_before_plane = from_behind(padded_state[:, -1:], "day", 1)
        apply_earlier = jnp.concatenate([apply_before_plane, padded_state[:, :-1]], 1)
        innovation = masked - forward_rows(apply_earlier, coefficients)
        weighted = precision * innovation
        weighted_padded = padded(weighted, (("space", 2),), 1)
        after_plane = from_behind(weighted_padded[:, :1], "day", -1)
        following = jnp.concatenate([weighted_padded[:, 1:], after_plane], 1)
        applied = weighted - transposed_rows(following, static_rim) + observed_precision * masked
        applied = sea_float * applied + (1.0 - sea_float) * direction
        curvature = lax.psum(local_sums(direction, applied), ("space", "day"))
        step_size = norm_now / curvature
        solution = solution + expand(step_size) * direction
        residual = residual - expand(step_size) * applied
        if iteration + 1 < ITERS:
            norm_next = residual_norms(residual)
            direction = residual + expand(norm_next / norm_now) * direction
            norm_now = norm_next
    samples = solution[1:]
    sample_padded = padded(samples, (("space", 2),), 1)
    before_plane = from_behind(sample_padded[:, -1:], "day", 1)
    earlier = jnp.concatenate([before_plane, sample_padded[:, :-1]], 1)
    centre = earlier[:, :, 1:-1]
    height = centre.shape[2]
    laplacian = -8.0 * centre
    for row_step, col_step in OFFSETS:
        if row_step != 0 or col_step != 0:
            laplacian = laplacian + column_shift(
                earlier[:, :, 1 + row_step : 1 + row_step + height], col_step
            )
    stacked = jnp.stack(
        [
            jnp.sum(centre * centre, axis=(0, 1)),
            jnp.sum(centre * laplacian, axis=(0, 1)),
            jnp.sum(laplacian * laplacian, axis=(0, 1)),
            jnp.sum(centre * samples, axis=(0, 1)),
            jnp.sum(laplacian * samples, axis=(0, 1)),
        ],
        0,
    )
    totals = lax.psum(stacked, "day")
    breadth = totals.shape[2] // day_total
    totals = lax.dynamic_slice_in_dim(totals, day_number * breadth, breadth, 2)
    return (solution[0], fit_cells(totals))


def solution(mesh):
    placed = (
        P("day", ("region", "space"), None),
        P("day", ("region", "space"), None),
        P(("region", "space"), None),
        P(None, ("region", "space"), None),
        P(("region", "space"), None),
        P(("region", "space"), None),
        P(None, "day", ("region", "space"), None),
    )
    return jax.shard_map(
        shards,
        mesh=mesh,
        in_specs=placed,
        out_specs=(P("day", ("region", "space"), None), P(None, ("region", "space"), "day")),
        check_vma=False,
    )
```

profile of v0, /device:TPU:0, one launch (start us, length us, event | category | flops | bytes accessed | tf_op | source)
XLA Modules:
  0.0 208.1 jit_solution(12920346424859504822)
XLA Ops:
  7.3 1.5 fusion.136
  8.8 1.3 collective-permute-start.4
  10.2 5.5 %collective-permute-start.3 = (f32[9,1,4096]{2,0,1:T(8,128)S(1)}, f32[9,1,4096]{2,0,1:T(8,128)S(1)}, u32[]{:S(2)}, u32[]{:S(2)}) collective-permute-start(f32[9,1,4096]{2,0,1:T(8,128)S(1)} %copy.10), channel_id=1, source_target_pairs={{0,2},{2,4},{4,6},{6,8},{8,10},{10,12},{12,14},{1,3},{3,5},{5,7},{... | collective-permute-start | bytes 442376 | tf_op jit(solution)/shard_map/ppermute | solution.py:18
  16.3 4.8 %collective-permute-start = (f32[3,2,1,4096]{3,2,1,0:T(1,128)S(1)}, f32[3,2,1,4096]{3,2,1,0:T(1,128)S(1)}, u32[]{:S(2)}, u32[]{:S(2)}) collective-permute-start(f32[3,2,1,4096]{3,2,1,0:T(1,128)S(1)} %get-tuple-element.83), channel_id=1, source_target_pairs={{0,2},{2,4},{4,6},{6,8},{8,10},{10,12},{12,14},{1,3},{3,5},{5,7},{... | collective-permute-start | bytes 294920 | tf_op jit(solution)/shard_map/ppermute | solution.py:18
  21.2 1.3 collective-permute-start.1
  22.6 7.4 %collective-permute-done = f32[3,2,1,4096]{3,2,1,0:T(1,128)S(1)} collective-permute-done((f32[3,2,1,4096]{3,2,1,0:T(1,128)S(1)}, f32[3,2,1,4096]{3,2,1,0:T(1,128)S(1)}, u32[]{:S(2)}, u32[]{:S(2)}) %collective-permute-start) | collective-permute-done | bytes 98336 | tf_op jit(solution)/shard_map/ppermute | solution.py:18
  30.3 1.9 collective-permute-start.2
  35.6 4.4 %collective-permute-start.5 = (f32[3,2,1,4096]{3,2,1,0:T(1,128)S(1)}, f32[3,2,1,4096]{3,2,1,0:T(1,128)S(1)}, u32[]{:S(2)}, u32[]{:S(2)}) collective-permute-start(f32[3,2,1,4096]{3,2,1,0:T(1,128)S(1)} %get-tuple-element.81), channel_id=1, source_target_pairs={{0,2},{2,4},{4,6},{6,8},{8,10},{10,12},{12,14},{1,3},{3,5},{5,7},{... | collective-permute-start | bytes 294920 | tf_op jit(solution)/shard_map/ppermute | solution.py:18
  40.0 1.3 collective-permute-start.6
  42.5 4.1 %collective-permute-done.6 = f32[3,2,1,4096]{3,2,1,0:T(1,128)S(1)} collective-permute-done((f32[3,2,1,4096]{3,2,1,0:T(1,128)S(1)}, f32[3,2,1,4096]{3,2,1,0:T(1,128)S(1)}, u32[]{:S(2)}, u32[]{:S(2)}) %collective-permute-start.6) | collective-permute-done | bytes 98336 | tf_op jit(solution)/shard_map/ppermute | solution.py:19
  47.0 1.3 collective-permute-start.7
  48.8 1.8 collective-permute-done.7
  52.6 30.4 %all-reduce.30 = (f32[3]{0:T(128)S(1)}, f32[3]{0:T(128)S(1)}) all-reduce(f32[3]{0:T(128)S(1)} %get-tuple-element.6, f32[3]{0:T(128)S(1)} %get-tuple-element.5), channel_id=1, replica_groups=mesh['region'=2,'space'=8,'day'=2] {'space','day'}, use_global_device_ids=true, to_apply=%region_1.0 | all-reduce | flops 6 | bytes 48 | tf_op jit(solution)/shard_map/psum | solution.py:95
  83.3 29.5 %psum.37 = f32[3]{0:T(128)S(1)} all-reduce(f32[3]{0:T(128)S(1)} %multiply_reduce_fusion), channel_id=1, replica_groups=mesh['region'=2,'space'=8,'day'=2] {'space','day'}, use_global_device_ids=true, to_apply=%region_5.0 | all-reduce | flops 3 | bytes 24 | tf_op jit(solution)/shard_map/psum | solution.py:95
  113.2 1.3 collective-permute-start.8
  114.5 1.3 collective-permute-start.9
  115.8 3.1 %collective-permute-done.8 = f32[3,2,1,4096]{3,2,1,0:T(1,128)S(1)} collective-permute-done((f32[3,2,1,4096]{3,2,1,0:T(1,128)S(1)}, f32[3,2,1,4096]{3,2,1,0:T(1,128)S(1)}, u32[]{:S(2)}, u32[]{:S(2)}) %collective-permute-start.8) | collective-permute-done | bytes 98336 | tf_op jit(solution)/shard_map/ppermute | solution.py:18
  119.0 2.1 collective-permute-done.9
  121.4 1.3 collective-permute-start.10
  122.7 1.3 collective-permute-done.10
  126.0 2.7 %collective-permute-start.11 = (f32[3,2,1,4096]{3,2,1,0:T(1,128)S(1)}, f32[3,2,1,4096]{3,2,1,0:T(1,128)S(1)}, u32[]{:S(2)}, u32[]{:S(2)}) collective-permute-start(f32[3,2,1,4096]{3,2,1,0:T(1,128)S(1)} %get-tuple-element.77), channel_id=1, source_target_pairs={{0,2},{2,4},{4,6},{6,8},{8,10},{10,12},{12,14},{1,3},{3,5},{5,7},{... | collective-permute-start | bytes 294920 | tf_op jit(solution)/shard_map/ppermute | solution.py:18
  128.7 1.3 collective-permute-start.12
  131.3 4.1 %collective-permute-done.12 = f32[3,2,1,4096]{3,2,1,0:T(1,128)S(1)} collective-permute-done((f32[3,2,1,4096]{3,2,1,0:T(1,128)S(1)}, f32[3,2,1,4096]{3,2,1,0:T(1,128)S(1)}, u32[]{:S(2)}, u32[]{:S(2)}) %collective-permute-start.12) | collective-permute-done | bytes 98336 | tf_op jit(solution)/shard_map/ppermute | solution.py:19
  135.7 1.5 collective-permute-start.13
  137.2 2.1 %collective-permute-done.13 = f32[3,1,6,4096]{3,2,1,0:T(8,128)S(1)} collective-permute-done((f32[3,1,6,4096]{3,2,1,0:T(8,128)S(1)}, f32[3,1,6,4096]{3,2,1,0:T(8,128)S(1)}, u32[]{:S(2)}, u32[]{:S(2)}) %collective-permute-start.13) | collective-permute-done | bytes 294944 | tf_op jit(solution)/shard_map/ppermute | solution.py:27
  141.2 29.7 %psum.38 = f32[3]{0:T(128)S(1)} all-reduce(f32[3]{0:T(128)S(1)} %fusion.103), channel_id=1, replica_groups=mesh['region'=2,'space'=8,'day'=2] {'space','day'}, use_global_device_ids=true, to_apply=%region_7.0 | all-reduce | flops 3 | bytes 24 | tf_op jit(solution)/shard_map/psum | solution.py:113
  171.2 1.3 collective-permute-start.14
  172.5 1.3 collective-permute-start.15
  173.8 1.5 collective-permute-done.14
  175.4 3.3 %collective-permute-done.15 = f32[2,2,1,4096]{3,2,1,0:T(1,128)S(1)} collective-permute-done((f32[2,2,1,4096]{3,2,1,0:T(1,128)S(1)}, f32[2,2,1,4096]{3,2,1,0:T(1,128)S(1)}, u32[]{:S(2)}, u32[]{:S(2)}) %collective-permute-start.15) | collective-permute-done | bytes 65568 | tf_op jit(solution)/shard_map/ppermute | solution.py:19
  178.9 1.3 collective-permute-start.16
  184.3 15.5 %all-reduce.33.cloned.1.call-done = f32[5,4,4096]{2,1,0:T(4,128)} async-done(((f32[5,4,4096]{2,1,0:T(4,128)}), f32[5,4,4096]{2,1,0:T(4,128)}) %all-reduce.33.cloned.1.call-update) | async-done | bytes 327696 | tf_op jit(solution)/shard_map/psum | solution.py:143
  (88 shorter events, 20.8 us)
Async XLA Ops:
  7.2 8.6 %copy-start.4 = (s32[4,4096]{1,0:T(4,128)S(1)}, s32[4,4096]{1,0:T(4,128)}, u32[]{:S(2)}) copy-start(s32[4,4096]{1,0:T(4,128)} %param.9) | copy-start | bytes 196612
  7.2 8.6 %copy-start.2 = (f32[2,4,4096]{2,1,0:T(4,128)S(1)}, f32[2,4,4096]{2,1,0:T(4,128)}, u32[]{:S(2)}) copy-start(f32[2,4,4096]{2,1,0:T(4,128)} %param.7) | copy-start | bytes 393220
  7.2 8.6 %copy-start.7 = (f32[4,4096]{1,0:T(4,128)S(1)}, f32[4,4096]{1,0:T(4,128)}, u32[]{:S(2)}) copy-start(f32[4,4096]{1,0:T(4,128)} %param.12) | copy-start | bytes 196612
  7.2 8.6 %copy-start.5 = (s32[2,4,4096]{2,1,0:T(4,128)S(1)}, s32[2,4,4096]{2,1,0:T(4,128)}, u32[]{:S(2)}) copy-start(s32[2,4,4096]{2,1,0:T(4,128)} %param.8) | copy-start | bytes 393220
  7.2 8.7 %copy-start.1 = (f32[4,4096]{1,0:T(4,128)S(1)}, f32[4,4096]{1,0:T(4,128)}, u32[]{:S(2)}) copy-start(f32[4,4096]{1,0:T(4,128)} %param.11) | copy-start | bytes 196612
  7.2 8.7 %copy-start.6 = (bf16[2,2,4,4096]{3,2,1,0:T(4,128)(2,1)S(1)}, bf16[2,2,4,4096]{3,2,1,0:T(4,128)(2,1)}, u32[]{:S(2)}) copy-start(bf16[2,2,4,4096]{3,2,1,0:T(4,128)(2,1)} %param.13) | copy-start | bytes 393220
  7.2 192.5 %all-reduce.33.cloned.1.call-start = ((), (), s32[]{:S(2)}) async-start(), calls=%async_computation | async-start | bytes 655360 | tf_op jit(solution)/shard_map/psum | solution.py:143
  8.8 23.4 %collective-permute-start.4 = (f32[9,1,4096]{2,0,1:T(8,128)S(1)}, f32[9,1,4096]{2,0,1:T(8,128)S(1)}, u32[]{:S(2)}, u32[]{:S(2)}) collective-permute-start(f32[9,1,4096]{2,0,1:T(8,128)S(1)} %copy.11), channel_id=1, source_target_pairs={{2,0},{4,2},{6,4},{8,6},{10,8},{12,10},{14,12},{3,1},{5,3},{7,5},{... | collective-permute-start | bytes 442376 | tf_op jit(solution)/shard_map/ppermute | solution.py:19
  10.2 22.2 %collective-permute-start.3 = (f32[9,1,4096]{2,0,1:T(8,128)S(1)}, f32[9,1,4096]{2,0,1:T(8,128)S(1)}, u32[]{:S(2)}, u32[]{:S(2)}) collective-permute-start(f32[9,1,4096]{2,0,1:T(8,128)S(1)} %copy.10), channel_id=1, source_target_pairs={{0,2},{2,4},{4,6},{6,8},{8,10},{10,12},{12,14},{1,3},{3,5},{5,7},{... | collective-permute-start | bytes 442376 | tf_op jit(solution)/shard_map/ppermute | solution.py:18
  15.9 6.6 %copy-start = (bf16[9,4,4096]{2,1,0:T(4,128)(2,1)S(1)}, bf16[9,4,4096]{2,1,0:T(4,128)(2,1)}, u32[]{:S(2)}) copy-start(bf16[9,4,4096]{2,1,0:T(4,128)(2,1)} %param.10) | copy-start | bytes 884740
  16.3 13.6 %collective-permute-start = (f32[3,2,1,4096]{3,2,1,0:T(1,128)S(1)}, f32[3,2,1,4096]{3,2,1,0:T(1,128)S(1)}, u32[]{:S(2)}, u32[]{:S(2)}) collective-permute-start(f32[3,2,1,4096]{3,2,1,0:T(1,128)S(1)} %get-tuple-element.83), channel_id=1, source_target_pairs={{0,2},{2,4},{4,6},{6,8},{8,10},{10,12},{12,14},{1,3},{3,5},{5,7},{... | collective-permute-start | bytes 294920 | tf_op jit(solution)/shard_map/ppermute | solution.py:18
  21.2 8.8 %collective-permute-start.1 = (f32[3,2,1,4096]{3,2,1,0:T(1,128)S(1)}, f32[3,2,1,4096]{3,2,1,0:T(1,128)S(1)}, u32[]{:S(2)}, u32[]{:S(2)}) collective-permute-start(f32[3,2,1,4096]{3,2,1,0:T(1,128)S(1)} %get-tuple-element.84), channel_id=1, source_target_pairs={{2,0},{4,2},{6,4},{8,6},{10,8},{12,10},{14,12},{3,1},{5,3},{7,5},{... | collective-permute-start | bytes 294920 | tf_op jit(solution)/shard_map/ppermute | solution.py:19
  30.3 3.3 %collective-permute-start.2 = (f32[3,1,6,4096]{3,2,1,0:T(8,128)S(1)}, f32[3,1,6,4096]{3,2,1,0:T(8,128)S(1)}, u32[]{:S(2)}, u32[]{:S(2)}) collective-permute-start(f32[3,1,6,4096]{3,2,1,0:T(8,128)S(1)} %get-tuple-element.56), channel_id=1, source_target_pairs={{0,1},{2,3},{4,5},{6,7},{8,9},{10,11},{12,13},{14,15},{16,17},{18,... | collective-permute-start | bytes 884744 | tf_op jit(solution)/shard_map/ppermute | solution.py:27
  35.6 7.0 %collective-permute-start.5 = (f32[3,2,1,4096]{3,2,1,0:T(1,128)S(1)}, f32[3,2,1,4096]{3,2,1,0:T(1,128)S(1)}, u32[]{:S(2)}, u32[]{:S(2)}) collective-permute-start(f32[3,2,1,4096]{3,2,1,0:T(1,128)S(1)} %get-tuple-element.81), channel_id=1, source_target_pairs={{0,2},{2,4},{4,6},{6,8},{8,10},{10,12},{12,14},{1,3},{3,5},{5,7},{... | collective-permute-start | bytes 294920 | tf_op jit(solution)/shard_map/ppermute | solution.py:18
  40.0 6.7 %collective-permute-start.6 = (f32[3,2,1,4096]{3,2,1,0:T(1,128)S(1)}, f32[3,2,1,4096]{3,2,1,0:T(1,128)S(1)}, u32[]{:S(2)}, u32[]{:S(2)}) collective-permute-start(f32[3,2,1,4096]{3,2,1,0:T(1,128)S(1)} %get-tuple-element.82), channel_id=1, source_target_pairs={{2,0},{4,2},{6,4},{8,6},{10,8},{12,10},{14,12},{3,1},{5,3},{7,5},{... | collective-permute-start | bytes 294920 | tf_op jit(solution)/shard_map/ppermute | solution.py:19
  47.0 3.6 %collective-permute-start.7 = (f32[3,1,6,4096]{3,2,1,0:T(8,128)S(1)}, f32[3,1,6,4096]{3,2,1,0:T(8,128)S(1)}, u32[]{:S(2)}, u32[]{:S(2)}) collective-permute-start(f32[3,1,6,4096]{3,2,1,0:T(8,128)S(1)} %get-tuple-element.49), channel_id=1, source_target_pairs={{1,0},{3,2},{5,4},{7,6},{9,8},{11,10},{13,12},{15,14},{17,16},{19,... | collective-permute-start | bytes 884744 | tf_op jit(solution)/shard_map/ppermute | solution.py:27
  113.2 5.7 %collective-permute-start.8 = (f32[3,2,1,4096]{3,2,1,0:T(1,128)S(1)}, f32[3,2,1,4096]{3,2,1,0:T(1,128)S(1)}, u32[]{:S(2)}, u32[]{:S(2)}) collective-permute-start(f32[3,2,1,4096]{3,2,1,0:T(1,128)S(1)} %get-tuple-element.79), channel_id=1, source_target_pairs={{0,2},{2,4},{4,6},{6,8},{8,10},{10,12},{12,14},{1,3},{3,5},{5,7},{... | collective-permute-start | bytes 294920 | tf_op jit(solution)/shard_map/ppermute | solution.py:18
  114.5 6.5 %collective-permute-start.9 = (f32[3,2,1,4096]{3,2,1,0:T(1,128)S(1)}, f32[3,2,1,4096]{3,2,1,0:T(1,128)S(1)}, u32[]{:S(2)}, u32[]{:S(2)}) collective-permute-start(f32[3,2,1,4096]{3,2,1,0:T(1,128)S(1)} %get-tuple-element.80), channel_id=1, source_target_pairs={{2,0},{4,2},{6,4},{8,6},{10,8},{12,10},{14,12},{3,1},{5,3},{7,5},{... | collective-permute-start | bytes 294920 | tf_op jit(solution)/shard_map/ppermute | solution.py:19
  121.4 2.6 %collective-permute-start.10 = (f32[3,1,6,4096]{3,2,1,0:T(8,128)S(1)}, f32[3,1,6,4096]{3,2,1,0:T(8,128)S(1)}, u32[]{:S(2)}, u32[]{:S(2)}) collective-permute-start(f32[3,1,6,4096]{3,2,1,0:T(8,128)S(1)} %get-tuple-element.41), channel_id=1, source_target_pairs={{0,1},{2,3},{4,5},{6,7},{8,9},{10,11},{12,13},{14,15},{16,17},{18,... | collective-permute-start | bytes 884744 | tf_op jit(solution)/shard_map/ppermute | solution.py:27
  126.0 5.3 %collective-permute-start.11 = (f32[3,2,1,4096]{3,2,1,0:T(1,128)S(1)}, f32[3,2,1,4096]{3,2,1,0:T(1,128)S(1)}, u32[]{:S(2)}, u32[]{:S(2)}) collective-permute-start(f32[3,2,1,4096]{3,2,1,0:T(1,128)S(1)} %get-tuple-element.77), channel_id=1, source_target_pairs={{0,2},{2,4},{4,6},{6,8},{8,10},{10,12},{12,14},{1,3},{3,5},{5,7},{... | collective-permute-start | bytes 294920 | tf_op jit(solution)/shard_map/ppermute | solution.py:18
  128.7 6.7 %collective-permute-start.12 = (f32[3,2,1,4096]{3,2,1,0:T(1,128)S(1)}, f32[3,2,1,4096]{3,2,1,0:T(1,128)S(1)}, u32[]{:S(2)}, u32[]{:S(2)}) collective-permute-start(f32[3,2,1,4096]{3,2,1,0:T(1,128)S(1)} %get-tuple-element.78), channel_id=1, source_target_pairs={{2,0},{4,2},{6,4},{8,6},{10,8},{12,10},{14,12},{3,1},{5,3},{7,5},{... | collective-permute-start | bytes 294920 | tf_op jit(solution)/shard_map/ppermute | solution.py:19
  135.7 3.6 %collective-permute-start.13 = (f32[3,1,6,4096]{3,2,1,0:T(8,128)S(1)}, f32[3,1,6,4096]{3,2,1,0:T(8,128)S(1)}, u32[]{:S(2)}, u32[]{:S(2)}) collective-permute-start(f32[3,1,6,4096]{3,2,1,0:T(8,128)S(1)} %get-tuple-element.34), channel_id=1, source_target_pairs={{1,0},{3,2},{5,4},{7,6},{9,8},{11,10},{13,12},{15,14},{17,16},{19,... | collective-permute-start | bytes 884744 | tf_op jit(solution)/shard_map/ppermute | solution.py:27
  171.2 4.1 %collective-permute-start.14 = (f32[2,2,1,4096]{3,2,1,0:T(1,128)S(1)}, f32[2,2,1,4096]{3,2,1,0:T(1,128)S(1)}, u32[]{:S(2)}, u32[]{:S(2)}) collective-permute-start(f32[2,2,1,4096]{3,2,1,0:T(1,128)S(1)} %get-tuple-element.75), channel_id=1, source_target_pairs={{0,2},{2,4},{4,6},{6,8},{8,10},{10,12},{12,14},{1,3},{3,5},{5,7},{... | collective-permute-start | bytes 196616 | tf_op jit(solution)/shard_map/ppermute | solution.py:18
  172.5 6.2 %collective-permute-start.15 = (f32[2,2,1,4096]{3,2,1,0:T(1,128)S(1)}, f32[2,2,1,4096]{3,2,1,0:T(1,128)S(1)}, u32[]{:S(2)}, u32[]{:S(2)}) collective-permute-start(f32[2,2,1,4096]{3,2,1,0:T(1,128)S(1)} %get-tuple-element.76), channel_id=1, source_target_pairs={{2,0},{4,2},{6,4},{8,6},{10,8},{12,10},{14,12},{3,1},{5,3},{7,5},{... | collective-permute-start | bytes 196616 | tf_op jit(solution)/shard_map/ppermute | solution.py:19
  178.9 2.4 %collective-permute-start.16 = (f32[2,1,6,4096]{3,2,1,0:T(8,128)S(1)}, f32[2,1,6,4096]{3,2,1,0:T(8,128)S(1)}, u32[]{:S(2)}, u32[]{:S(2)}) collective-permute-start(f32[2,1,6,4096]{3,2,1,0:T(8,128)S(1)} %get-tuple-element.72), channel_id=1, source_target_pairs={{0,1},{2,3},{4,5},{6,7},{8,9},{10,11},{12,13},{14,15},{16,17},{18,... | collective-permute-start | bytes 589832 | tf_op jit(solution)/shard_map/ppermute | solution.py:27
  182.8 0.7 copy-start.3
Sparse Core Ops, SparseCore 0:
  183.7 15.9 all-reduce.32
where the time goes:
time: 209 us; the launch traced here: 208 us
  blocking collectives  89.6 us (43%)
  waiting for transfers between devices  50.6 us (24%)
  starting transfers between devices  35.2 us (17%)
  between operations  14.7 us (7%)
  other arithmetic  13.1 us (6%)
  local copies, waits for them, and re-layouts  4.99 us (2%)
    psum x2, blocking collectives, residual_norms(): return lax.psum(local_sums(residual, residual), ('space', 'day'))  59.9 us
    psum x1, blocking collectives, shards(): curvature = lax.psum(local_sums(direction, applied), ('space', 'day'))  29.7 us
    ppermute x6, starting transfers between devices, padded(): before = lax.ppermute(last, axis, up)  20 us
    psum x1, waiting for transfers between devices, shards(): totals = lax.psum(stacked, 'day')  15.5 us
    ppermute x6, waiting for transfers between devices, padded(): before = lax.ppermute(last, axis, up)  14.2 us
    ppermute x6, waiting for transfers between devices, padded(): after = lax.ppermute(first, axis, down)  13.6 us
    ppermute x6, starting transfers between devices, padded(): after = lax.ppermute(first, axis, down)  7.75 us
    ppermute x5, starting transfers between devices, from_behind(): return lax.ppermute(x, axis, pairs)  7.33 us
  transfers between devices with their start and end apart: 18, of which 15 were waited for; matrix products, arithmetic and copies ran while one was open for 1% of the time, Pallas kernels for 0%

commit v1 on v0

--- a/solution.py
+++ b/solution.py
@@ -92,7 +92,10 @@
     day_total = lax.axis_size("day")
 
     def residual_norms(residual):
-        return lax.psum(local_sums(residual, residual), ("space", "day"))
+        plan_blocks = lambda frame, net_axis, link_axis: lax.psum(
+            lax.psum(frame, net_axis), link_axis
+        )
+        return plan_blocks(local_sums(residual, residual), "day", "space")
 
     solution = jnp.zeros_like(right_sides)
     residual = right_sides

time: 209 us -> 221 us (1.057)
  blocking collectives: 89.6 us -> 101 us
    psum x1 -> x2, blocking collectives: 29.7 us -> 60.1 us  [shards(): curvature = lax.psum(local_sums(direction, applied), ('space', 'day'))]
    psum x2 -> x4, blocking collectives: 59.9 us -> 41.1 us  [the longest x2 36.2 us: residual_norms(): lax.psum(lax.psum(frame, net_axis), link_axis)]
where the time goes in v1:
time: 221 us; the launch traced here: 220 us
  blocking collectives  101 us (46%)
  waiting for transfers between devices  50.5 us (23%)
  starting transfers between devices  36.1 us (16%)
  between operations  14.7 us (7%)
  other arithmetic  13.1 us (6%)
  local copies, waits for them, and re-layouts  4.98 us (2%)
    psum x2, blocking collectives, shards(): curvature = lax.psum(local_sums(direction, applied), ('space', 'day'))  60.1 us
    psum x2, blocking collectives, residual_norms(): lax.psum(lax.psum(frame, net_axis), link_axis)  36.2 us
    ppermute x6, starting transfers between devices, padded(): before = lax.ppermute(last, axis, up)  21 us
    ppermute x6, waiting for transfers between devices, padded(): after = lax.ppermute(first, axis, down)  15.8 us
    psum x1, waiting for transfers between devices, shards(): totals = lax.psum(stacked, 'day')  15.4 us
    ppermute x6, waiting for transfers between devices, padded(): before = lax.ppermute(last, axis, up)  12 us
    ppermute x6, starting transfers between devices, padded(): after = lax.ppermute(first, axis, down)  7.75 us
    ppermute x5, starting transfers between devices, from_behind(): return lax.ppermute(x, axis, pairs)  7.33 us
  transfers between devices with their start and end apart: 18, of which 15 were waited for; matrix products, arithmetic and copies ran while one was open for 1% of the time, Pallas kernels for 0%

profile of v1, /device:TPU:0, one launch (start us, length us, event | category | flops | bytes accessed | tf_op | source)
XLA Modules:
  0.0 220.5 jit_solution(10167833488906694603)
XLA Ops:
  7.3 1.5 fusion.136
  8.8 1.3 collective-permute-start.4
  10.2 5.5 %collective-permute-start.3 = (f32[9,1,4096]{2,0,1:T(8,128)S(1)}, f32[9,1,4096]{2,0,1:T(8,128)S(1)}, u32[]{:S(2)}, u32[]{:S(2)}) collective-permute-start(f32[9,1,4096]{2,0,1:T(8,128)S(1)} %copy.10), channel_id=1, source_target_pairs={{0,2},{2,4},{4,6},{6,8},{8,10},{10,12},{12,14},{1,3},{3,5},{5,7},{... | collective-permute-start | bytes 442376 | tf_op jit(solution)/shard_map/ppermute | solution.py:18
  16.3 4.8 %collective-permute-start = (f32[3,2,1,4096]{3,2,1,0:T(1,128)S(1)}, f32[3,2,1,4096]{3,2,1,0:T(1,128)S(1)}, u32[]{:S(2)}, u32[]{:S(2)}) collective-permute-start(f32[3,2,1,4096]{3,2,1,0:T(1,128)S(1)} %get-tuple-element.81), channel_id=1, source_target_pairs={{0,2},{2,4},{4,6},{6,8},{8,10},{10,12},{12,14},{1,3},{3,5},{5,7},{... | collective-permute-start | bytes 294920 | tf_op jit(solution)/shard_map/ppermute | solution.py:18
  21.2 1.3 collective-permute-start.1
  22.6 7.4 %collective-permute-done = f32[3,2,1,4096]{3,2,1,0:T(1,128)S(1)} collective-permute-done((f32[3,2,1,4096]{3,2,1,0:T(1,128)S(1)}, f32[3,2,1,4096]{3,2,1,0:T(1,128)S(1)}, u32[]{:S(2)}, u32[]{:S(2)}) %collective-permute-start) | collective-permute-done | bytes 98336 | tf_op jit(solution)/shard_map/ppermute | solution.py:18
  30.3 1.9 collective-permute-start.2
  35.6 4.4 %collective-permute-start.5 = (f32[3,2,1,4096]{3,2,1,0:T(1,128)S(1)}, f32[3,2,1,4096]{3,2,1,0:T(1,128)S(1)}, u32[]{:S(2)}, u32[]{:S(2)}) collective-permute-start(f32[3,2,1,4096]{3,2,1,0:T(1,128)S(1)} %get-tuple-element.79), channel_id=1, source_target_pairs={{0,2},{2,4},{4,6},{6,8},{8,10},{10,12},{12,14},{1,3},{3,5},{5,7},{... | collective-permute-start | bytes 294920 | tf_op jit(solution)/shard_map/ppermute | solution.py:18
  40.0 1.3 collective-permute-start.6
  42.5 4.1 %collective-permute-done.6 = f32[3,2,1,4096]{3,2,1,0:T(1,128)S(1)} collective-permute-done((f32[3,2,1,4096]{3,2,1,0:T(1,128)S(1)}, f32[3,2,1,4096]{3,2,1,0:T(1,128)S(1)}, u32[]{:S(2)}, u32[]{:S(2)}) %collective-permute-start.6) | collective-permute-done | bytes 98336 | tf_op jit(solution)/shard_map/ppermute | solution.py:19
  48.8 1.8 collective-permute-done.7
  52.6 2.5 %psum.49 = f32[3]{0:T(128)S(1)} all-reduce(f32[3]{0:T(128)S(1)} %get-tuple-element.6), channel_id=1, replica_groups=mesh['region'=2,'space'=8,'day'=2] {'day'}, use_global_device_ids=true, to_apply=%region_1.0 | all-reduce | flops 3 | bytes 24 | tf_op jit(solution)/shard_map/psum | solution.py:96
  55.0 30.5 %psum.51 = f32[3]{0:T(128)S(1)} all-reduce(f32[3]{0:T(128)S(1)} %get-tuple-element.5), channel_id=1, replica_groups=mesh['region'=2,'space'=8,'day'=2] {'space','day'}, use_global_device_ids=true, to_apply=%region_4.0 | all-reduce | flops 3 | bytes 24 | tf_op jit(solution)/shard_map/psum | solution.py:116
  85.5 17.1 %psum.50 = f32[3]{0:T(128)S(1)} all-reduce(f32[3]{0:T(128)S(1)} %psum.49), channel_id=1, replica_groups=mesh['region'=2,'space'=8,'day'=2] {'space'}, use_global_device_ids=true, to_apply=%region_2.0 | all-reduce | flops 3 | bytes 24 | tf_op jit(solution)/shard_map/psum | solution.py:95
  102.9 2.4 %psum.52 = f32[3]{0:T(128)S(1)} all-reduce(f32[3]{0:T(128)S(1)} %multiply_reduce_fusion), channel_id=1, replica_groups=mesh['region'=2,'space'=8,'day'=2] {'day'}, use_global_device_ids=true, to_apply=%region_6.0 | all-reduce | flops 3 | bytes 24 | tf_op jit(solution)/shard_map/psum | solution.py:96
  105.4 19.1 %psum.53 = f32[3]{0:T(128)S(1)} all-reduce(f32[3]{0:T(128)S(1)} %psum.52), channel_id=1, replica_groups=mesh['region'=2,'space'=8,'day'=2] {'space'}, use_global_device_ids=true, to_apply=%region_7.0 | all-reduce | flops 3 | bytes 24 | tf_op jit(solution)/shard_map/psum | solution.py:95
  124.9 1.9 collective-permute-start.8
  129.0 4.3 %collective-permute-done.9 = f32[3,2,1,4096]{3,2,1,0:T(1,128)S(1)} collective-permute-done((f32[3,2,1,4096]{3,2,1,0:T(1,128)S(1)}, f32[3,2,1,4096]{3,2,1,0:T(1,128)S(1)}, u32[]{:S(2)}, u32[]{:S(2)}) %collective-permute-start.9) | collective-permute-done | bytes 98336 | tf_op jit(solution)/shard_map/ppermute | solution.py:19
  133.7 1.3 collective-permute-start.10
  135.0 1.3 collective-permute-done.10
  138.3 3.0 %collective-permute-start.11 = (f32[3,2,1,4096]{3,2,1,0:T(1,128)S(1)}, f32[3,2,1,4096]{3,2,1,0:T(1,128)S(1)}, u32[]{:S(2)}, u32[]{:S(2)}) collective-permute-start(f32[3,2,1,4096]{3,2,1,0:T(1,128)S(1)} %get-tuple-element.75), channel_id=1, source_target_pairs={{0,2},{2,4},{4,6},{6,8},{8,10},{10,12},{12,14},{1,3},{3,5},{5,7},{... | collective-permute-start | bytes 294920 | tf_op jit(solution)/shard_map/ppermute | solution.py:18
  141.3 1.3 collective-permute-start.12
  143.9 4.1 %collective-permute-done.12 = f32[3,2,1,4096]{3,2,1,0:T(1,128)S(1)} collective-permute-done((f32[3,2,1,4096]{3,2,1,0:T(1,128)S(1)}, f32[3,2,1,4096]{3,2,1,0:T(1,128)S(1)}, u32[]{:S(2)}, u32[]{:S(2)}) %collective-permute-start.12) | collective-permute-done | bytes 98336 | tf_op jit(solution)/shard_map/ppermute | solution.py:19
  148.3 1.5 collective-permute-start.13
  149.8 2.1 collective-permute-done.13
  153.8 29.6 %psum.54 = f32[3]{0:T(128)S(1)} all-reduce(f32[3]{0:T(128)S(1)} %fusion.103), channel_id=1, replica_groups=mesh['region'=2,'space'=8,'day'=2] {'space','day'}, use_global_device_ids=true, to_apply=%region_9.0 | all-reduce | flops 3 | bytes 24 | tf_op jit(solution)/shard_map/psum | solution.py:116
  183.7 1.3 collective-permute-start.14
  185.0 1.3 collective-permute-start.15
  186.3 1.6 collective-permute-done.14
  188.0 3.2 %collective-permute-done.15 = f32[2,2,1,4096]{3,2,1,0:T(1,128)S(1)} collective-permute-done((f32[2,2,1,4096]{3,2,1,0:T(1,128)S(1)}, f32[2,2,1,4096]{3,2,1,0:T(1,128)S(1)}, u32[]{:S(2)}, u32[]{:S(2)}) %collective-permute-start.15) | collective-permute-done | bytes 65568 | tf_op jit(solution)/shard_map/ppermute | solution.py:19
  191.4 1.3 collective-permute-start.16
  196.8 15.4 %all-reduce.32.cloned.1.call-done = f32[5,4,4096]{2,1,0:T(4,128)} async-done(((f32[5,4,4096]{2,1,0:T(4,128)}), f32[5,4,4096]{2,1,0:T(4,128)}) %all-reduce.32.cloned.1.call-update) | async-done | bytes 327696 | tf_op jit(solution)/shard_map/psum | solution.py:146
  (91 shorter events, 24.3 us)
Async XLA Ops:
  7.2 8.6 %copy-start.4 = (s32[4,4096]{1,0:T(4,128)S(1)}, s32[4,4096]{1,0:T(4,128)}, u32[]{:S(2)}) copy-start(s32[4,4096]{1,0:T(4,128)} %param.9) | copy-start | bytes 196612
  7.2 8.6 %copy-start.2 = (f32[2,4,4096]{2,1,0:T(4,128)S(1)}, f32[2,4,4096]{2,1,0:T(4,128)}, u32[]{:S(2)}) copy-start(f32[2,4,4096]{2,1,0:T(4,128)} %param.7) | copy-start | bytes 393220
  7.2 8.6 %copy-start.7 = (f32[4,4096]{1,0:T(4,128)S(1)}, f32[4,4096]{1,0:T(4,128)}, u32[]{:S(2)}) copy-start(f32[4,4096]{1,0:T(4,128)} %param.12) | copy-start | bytes 196612
  7.2 8.6 %copy-start.5 = (s32[2,4,4096]{2,1,0:T(4,128)S(1)}, s32[2,4,4096]{2,1,0:T(4,128)}, u32[]{:S(2)}) copy-start(s32[2,4,4096]{2,1,0:T(4,128)} %param.8) | copy-start | bytes 393220
  7.2 8.7 %copy-start.1 = (f32[4,4096]{1,0:T(4,128)S(1)}, f32[4,4096]{1,0:T(4,128)}, u32[]{:S(2)}) copy-start(f32[4,4096]{1,0:T(4,128)} %param.11) | copy-start | bytes 196612
  7.2 8.7 %copy-start.6 = (bf16[2,2,4,4096]{3,2,1,0:T(4,128)(2,1)S(1)}, bf16[2,2,4,4096]{3,2,1,0:T(4,128)(2,1)}, u32[]{:S(2)}) copy-start(bf16[2,2,4,4096]{3,2,1,0:T(4,128)(2,1)} %param.13) | copy-start | bytes 393220
  7.2 204.9 %all-reduce.32.cloned.1.call-start = ((), (), s32[]{:S(2)}) async-start(), calls=%async_computation | async-start | bytes 655360 | tf_op jit(solution)/shard_map/psum | solution.py:146
  8.8 23.4 %collective-permute-start.4 = (f32[9,1,4096]{2,0,1:T(8,128)S(1)}, f32[9,1,4096]{2,0,1:T(8,128)S(1)}, u32[]{:S(2)}, u32[]{:S(2)}) collective-permute-start(f32[9,1,4096]{2,0,1:T(8,128)S(1)} %copy.11), channel_id=1, source_target_pairs={{2,0},{4,2},{6,4},{8,6},{10,8},{12,10},{14,12},{3,1},{5,3},{7,5},{... | collective-permute-start | bytes 442376 | tf_op jit(solution)/shard_map/ppermute | solution.py:19
  10.2 22.2 %collective-permute-start.3 = (f32[9,1,4096]{2,0,1:T(8,128)S(1)}, f32[9,1,4096]{2,0,1:T(8,128)S(1)}, u32[]{:S(2)}, u32[]{:S(2)}) collective-permute-start(f32[9,1,4096]{2,0,1:T(8,128)S(1)} %copy.10), channel_id=1, source_target_pairs={{0,2},{2,4},{4,6},{6,8},{8,10},{10,12},{12,14},{1,3},{3,5},{5,7},{... | collective-permute-start | bytes 442376 | tf_op jit(solution)/shard_map/ppermute | solution.py:18
  15.9 6.6 %copy-start = (bf16[9,4,4096]{2,1,0:T(4,128)(2,1)S(1)}, bf16[9,4,4096]{2,1,0:T(4,128)(2,1)}, u32[]{:S(2)}) copy-start(bf16[9,4,4096]{2,1,0:T(4,128)(2,1)} %param.10) | copy-start | bytes 884740
  16.3 13.6 %collective-permute-start = (f32[3,2,1,4096]{3,2,1,0:T(1,128)S(1)}, f32[3,2,1,4096]{3,2,1,0:T(1,128)S(1)}, u32[]{:S(2)}, u32[]{:S(2)}) collective-permute-start(f32[3,2,1,4096]{3,2,1,0:T(1,128)S(1)} %get-tuple-element.81), channel_id=1, source_target_pairs={{0,2},{2,4},{4,6},{6,8},{8,10},{10,12},{12,14},{1,3},{3,5},{5,7},{... | collective-permute-start | bytes 294920 | tf_op jit(solution)/shard_map/ppermute | solution.py:18
  21.2 8.8 %collective-permute-start.1 = (f32[3,2,1,4096]{3,2,1,0:T(1,128)S(1)}, f32[3,2,1,4096]{3,2,1,0:T(1,128)S(1)}, u32[]{:S(2)}, u32[]{:S(2)}) collective-permute-start(f32[3,2,1,4096]{3,2,1,0:T(1,128)S(1)} %get-tuple-element.82), channel_id=1, source_target_pairs={{2,0},{4,2},{6,4},{8,6},{10,8},{12,10},{14,12},{3,1},{5,3},{7,5},{... | collective-permute-start | bytes 294920 | tf_op jit(solution)/shard_map/ppermute | solution.py:19
  30.3 3.3 %collective-permute-start.2 = (f32[3,1,6,4096]{3,2,1,0:T(8,128)S(1)}, f32[3,1,6,4096]{3,2,1,0:T(8,128)S(1)}, u32[]{:S(2)}, u32[]{:S(2)}) collective-permute-start(f32[3,1,6,4096]{3,2,1,0:T(8,128)S(1)} %get-tuple-element.54), channel_id=1, source_target_pairs={{0,1},{2,3},{4,5},{6,7},{8,9},{10,11},{12,13},{14,15},{16,17},{18,... | collective-permute-start | bytes 884744 | tf_op jit(solution)/shard_map/ppermute | solution.py:27
  35.6 7.0 %collective-permute-start.5 = (f32[3,2,1,4096]{3,2,1,0:T(1,128)S(1)}, f32[3,2,1,4096]{3,2,1,0:T(1,128)S(1)}, u32[]{:S(2)}, u32[]{:S(2)}) collective-permute-start(f32[3,2,1,4096]{3,2,1,0:T(1,128)S(1)} %get-tuple-element.79), channel_id=1, source_target_pairs={{0,2},{2,4},{4,6},{6,8},{8,10},{10,12},{12,14},{1,3},{3,5},{5,7},{... | collective-permute-start | bytes 294920 | tf_op jit(solution)/shard_map/ppermute | solution.py:18
  40.0 6.7 %collective-permute-start.6 = (f32[3,2,1,4096]{3,2,1,0:T(1,128)S(1)}, f32[3,2,1,4096]{3,2,1,0:T(1,128)S(1)}, u32[]{:S(2)}, u32[]{:S(2)}) collective-permute-start(f32[3,2,1,4096]{3,2,1,0:T(1,128)S(1)} %get-tuple-element.80), channel_id=1, source_target_pairs={{2,0},{4,2},{6,4},{8,6},{10,8},{12,10},{14,12},{3,1},{5,3},{7,5},{... | collective-permute-start | bytes 294920 | tf_op jit(solution)/shard_map/ppermute | solution.py:19
  47.0 3.6 %collective-permute-start.7 = (f32[3,1,6,4096]{3,2,1,0:T(8,128)S(1)}, f32[3,1,6,4096]{3,2,1,0:T(8,128)S(1)}, u32[]{:S(2)}, u32[]{:S(2)}) collective-permute-start(f32[3,1,6,4096]{3,2,1,0:T(8,128)S(1)} %get-tuple-element.47), channel_id=1, source_target_pairs={{1,0},{3,2},{5,4},{7,6},{9,8},{11,10},{13,12},{15,14},{17,16},{19,... | collective-permute-start | bytes 884744 | tf_op jit(solution)/shard_map/ppermute | solution.py:27
  124.9 4.1 %collective-permute-start.8 = (f32[3,2,1,4096]{3,2,1,0:T(1,128)S(1)}, f32[3,2,1,4096]{3,2,1,0:T(1,128)S(1)}, u32[]{:S(2)}, u32[]{:S(2)}) collective-permute-start(f32[3,2,1,4096]{3,2,1,0:T(1,128)S(1)} %get-tuple-element.77), channel_id=1, source_target_pairs={{0,2},{2,4},{4,6},{6,8},{8,10},{10,12},{12,14},{1,3},{3,5},{5,7},{... | collective-permute-start | bytes 294920 | tf_op jit(solution)/shard_map/ppermute | solution.py:18
  126.8 6.5 %collective-permute-start.9 = (f32[3,2,1,4096]{3,2,1,0:T(1,128)S(1)}, f32[3,2,1,4096]{3,2,1,0:T(1,128)S(1)}, u32[]{:S(2)}, u32[]{:S(2)}) collective-permute-start(f32[3,2,1,4096]{3,2,1,0:T(1,128)S(1)} %get-tuple-element.78), channel_id=1, source_target_pairs={{2,0},{4,2},{6,4},{8,6},{10,8},{12,10},{14,12},{3,1},{5,3},{7,5},{... | collective-permute-start | bytes 294920 | tf_op jit(solution)/shard_map/ppermute | solution.py:19
  133.7 2.6 %collective-permute-start.10 = (f32[3,1,6,4096]{3,2,1,0:T(8,128)S(1)}, f32[3,1,6,4096]{3,2,1,0:T(8,128)S(1)}, u32[]{:S(2)}, u32[]{:S(2)}) collective-permute-start(f32[3,1,6,4096]{3,2,1,0:T(8,128)S(1)} %get-tuple-element.39), channel_id=1, source_target_pairs={{0,1},{2,3},{4,5},{6,7},{8,9},{10,11},{12,13},{14,15},{16,17},{18,... | collective-permute-start | bytes 884744 | tf_op jit(solution)/shard_map/ppermute | solution.py:27
  138.3 5.6 %collective-permute-start.11 = (f32[3,2,1,4096]{3,2,1,0:T(1,128)S(1)}, f32[3,2,1,4096]{3,2,1,0:T(1,128)S(1)}, u32[]{:S(2)}, u32[]{:S(2)}) collective-permute-start(f32[3,2,1,4096]{3,2,1,0:T(1,128)S(1)} %get-tuple-element.75), channel_id=1, source_target_pairs={{0,2},{2,4},{4,6},{6,8},{8,10},{10,12},{12,14},{1,3},{3,5},{5,7},{... | collective-permute-start | bytes 294920 | tf_op jit(solution)/shard_map/ppermute | solution.py:18
  141.3 6.7 %collective-permute-start.12 = (f32[3,2,1,4096]{3,2,1,0:T(1,128)S(1)}, f32[3,2,1,4096]{3,2,1,0:T(1,128)S(1)}, u32[]{:S(2)}, u32[]{:S(2)}) collective-permute-start(f32[3,2,1,4096]{3,2,1,0:T(1,128)S(1)} %get-tuple-element.76), channel_id=1, source_target_pairs={{2,0},{4,2},{6,4},{8,6},{10,8},{12,10},{14,12},{3,1},{5,3},{7,5},{... | collective-permute-start | bytes 294920 | tf_op jit(solution)/shard_map/ppermute | solution.py:19
  148.3 3.6 %collective-permute-start.13 = (f32[3,1,6,4096]{3,2,1,0:T(8,128)S(1)}, f32[3,1,6,4096]{3,2,1,0:T(8,128)S(1)}, u32[]{:S(2)}, u32[]{:S(2)}) collective-permute-start(f32[3,1,6,4096]{3,2,1,0:T(8,128)S(1)} %get-tuple-element.32), channel_id=1, source_target_pairs={{1,0},{3,2},{5,4},{7,6},{9,8},{11,10},{13,12},{15,14},{17,16},{19,... | collective-permute-start | bytes 884744 | tf_op jit(solution)/shard_map/ppermute | solution.py:27
  183.7 4.2 %collective-permute-start.14 = (f32[2,2,1,4096]{3,2,1,0:T(1,128)S(1)}, f32[2,2,1,4096]{3,2,1,0:T(1,128)S(1)}, u32[]{:S(2)}, u32[]{:S(2)}) collective-permute-start(f32[2,2,1,4096]{3,2,1,0:T(1,128)S(1)} %get-tuple-element.73), channel_id=1, source_target_pairs={{0,2},{2,4},{4,6},{6,8},{8,10},{10,12},{12,14},{1,3},{3,5},{5,7},{... | collective-permute-start | bytes 196616 | tf_op jit(solution)/shard_map/ppermute | solution.py:18
  185.0 6.2 %collective-permute-start.15 = (f32[2,2,1,4096]{3,2,1,0:T(1,128)S(1)}, f32[2,2,1,4096]{3,2,1,0:T(1,128)S(1)}, u32[]{:S(2)}, u32[]{:S(2)}) collective-permute-start(f32[2,2,1,4096]{3,2,1,0:T(1,128)S(1)} %get-tuple-element.74), channel_id=1, source_target_pairs={{2,0},{4,2},{6,4},{8,6},{10,8},{12,10},{14,12},{3,1},{5,3},{7,5},{... | collective-permute-start | bytes 196616 | tf_op jit(solution)/shard_map/ppermute | solution.py:19
  191.4 2.4 %collective-permute-start.16 = (f32[2,1,6,4096]{3,2,1,0:T(8,128)S(1)}, f32[2,1,6,4096]{3,2,1,0:T(8,128)S(1)}, u32[]{:S(2)}, u32[]{:S(2)}) collective-permute-start(f32[2,1,6,4096]{3,2,1,0:T(8,128)S(1)} %get-tuple-element.70), channel_id=1, source_target_pairs={{0,1},{2,3},{4,5},{6,7},{8,9},{10,11},{12,13},{14,15},{16,17},{18,... | collective-permute-start | bytes 589832 | tf_op jit(solution)/shard_map/ppermute | solution.py:27
  195.3 0.7 copy-start.3
Sparse Core Ops, SparseCore 0:
  196.2 15.8 all-reduce.31
